TPU v7x, 256 devices: a whole 4x4x8 slice. The times are simulated.
256 devices in a mesh: seq: 16 (over y, z_hi), fsdp: 16 (over x, z_lo, core).
Axes of the slice: x: 4, y: 4, z: 8 (z_hi: 4, z_lo: 2; z = z_hi * 2 + z_lo), core: 2. Of those that a mesh axis runs over, the one named last changes fastest.
Arguments:
- tokens: bfloat16 [2048, 4096], P('seq', 'fsdp'), may hold values from -6 to 6
- in_weight: bfloat16 [3, 4096, 4096], P(None, 'seq', 'fsdp'), may hold values from -0.09375 to 0.09375
- out_weight: bfloat16 [4096, 4096], P('fsdp', 'seq'), may hold values from -0.09375 to 0.09375
- filters: float32 [4096, 128], P('fsdp'), may hold values from -0.5 to 0.5
- cotangent: bfloat16 [2048, 4096], P('seq', 'fsdp'), may hold values from -6 to 6
Outputs:
- mixed_out: bfloat16 [2048, 4096], P('seq', 'fsdp')
- grad_tokens: bfloat16 [2048, 4096], P('seq', 'fsdp')
- grad_in_weight: float32 [3, 4096, 4096], P(None, 'seq', 'fsdp')
- grad_out_weight: float32 [4096, 4096], P('fsdp', 'seq')
- grad_filters: float32 [4096, 128], P('fsdp')
All inputs are finite; a program needn't handle non-finite values.
Results may differ from a plain program's by a relative error of at most 0.018.
Values may be sent and summed in bfloat16 or wider, within the bound.
A program may use at most 64 MiB of HBM per device.

v0:
```python
import jax
import jax.numpy as jnp
from jax import lax
from jax.sharding import PartitionSpec as P

highest = lax.Precision.HIGHEST


def from_behind(value, axis, by):
    length = lax.axis_size(axis)
    pairs = [(i, i + by) for i in range(length) if 0 <= i + by < length]
    return lax.ppermute(value, axis, pairs)


def causal_filter(extended, filters):
    kernel = jnp.flip(jnp.transpose(filters), 0)[:, None, :]
    result = lax.conv_general_dilated(
        extended[None],
        kernel,
        (1,),
        "VALID",
        dimension_numbers=("NWC", "WIO", "NWC"),
        feature_group_count=filters.shape[0],
        precision=highest,
    )
    return result[0]


def reverse_filter(extended, filters):
    kernel = jnp.transpose(filters)[:, None, :]
    result = lax.conv_general_dilated(
        extended[None],
        kernel,
        (1,),
        "VALID",
        dimension_numbers=("NWC", "WIO", "NWC"),
        feature_group_count=filters.shape[0],
        precision=highest,
    )
    return result[0]


def filter_grad(extended, gradient):
    result = lax.conv_general_dilated(
        extended[None],
        gradient[:, None, :],
        (1,),
        "VALID",
        dimension_numbers=("NWC", "WIO", "NWC"),
        feature_group_count=gradient.shape[1],
        precision=highest,
    )
    return jnp.transpose(jnp.flip(result[0], 0))


def on_device(tokens, in_weight, out_weight, filters, cotangent):
    margin = filters.shape[1] - 1
    gathered = lax.all_gather(tokens, "fsdp", axis=1, tiled=True)
    out_full = lax.all_gather(out_weight, "seq", axis=1, tiled=True)
    in_full = lax.all_gather(in_weight, "seq", axis=1, tiled=True)
    projected = jnp.einsum("td,idc->itc", gathered, in_full, preferred_element_type=jnp.float32)
    projected = projected.astype(jnp.bfloat16)
    queries = projected[0].astype(jnp.float32)
    key_part = projected[1].astype(jnp.float32)
    value_part = projected[2].astype(jnp.float32)
    signal = (key_part * value_part).astype(jnp.bfloat16)
    earlier = from_behind(signal[-margin:], "seq", 1)
    extended = jnp.concatenate([earlier, signal], 0).astype(jnp.float32)
    filtered = causal_filter(extended, filters)
    gated_rows = (queries * filtered).astype(jnp.bfloat16)
    partial_value = jnp.dot(gated_rows, out_full, preferred_element_type=jnp.float32)
    mixed_out = lax.psum_scatter(
        partial_value.astype(jnp.bfloat16), "fsdp", scatter_dimension=1, tiled=True
    )
    grad_full = lax.all_gather(cotangent, "fsdp", axis=1, tiled=True)
    grad_gated = lax.dot_general(
        grad_full, out_full, (((1,), (1,)), ((), ())), preferred_element_type=jnp.float32
    )
    grad_queries = grad_gated * filtered
    grad_filtered = (grad_gated * queries).astype(jnp.bfloat16)
    later_rows = from_behind(grad_filtered[:margin], "seq", -1)
    grad_signal = reverse_filter(
        jnp.concatenate([grad_filtered, later_rows], 0).astype(jnp.float32), filters
    )
    grad_filters = lax.psum(
        filter_grad(extended, grad_filtered.astype(jnp.float32)).astype(jnp.bfloat16), "seq"
    ).astype(jnp.float32)
    grad_projected = jnp.stack(
        [grad_queries, grad_signal * value_part, grad_signal * key_part]
    ).astype(jnp.bfloat16)
    grad_partial = jnp.einsum(
        "itc,idc->td", grad_projected, in_full, preferred_element_type=jnp.float32
    )
    grad_tokens = lax.psum_scatter(
        grad_partial.astype(jnp.bfloat16), "fsdp", scatter_dimension=1, tiled=True
    )
    weight_in_part = jnp.einsum(
        "td,itc->idc", gathered, grad_projected, preferred_element_type=jnp.float32
    )
    weight_out_part = lax.dot_general(
        gated_rows, grad_full, (((0,), (0,)), ((), ())), preferred_element_type=jnp.float32
    )
    grad_in_weight, grad_out_weight = (
        lax.psum_scatter(
            weight_in_part.astype(jnp.bfloat16), "seq", scatter_dimension=1, tiled=True
        ).astype(jnp.float32),
        lax.psum_scatter(
            weight_out_part.astype(jnp.bfloat16), "seq", scatter_dimension=1, tiled=True
        ).astype(jnp.float32),
    )
    return (mixed_out, grad_tokens, grad_in_weight, grad_out_weight, grad_filters)


def solution(mesh):
    placed = (
        P("seq", "fsdp"),
        P(None, "seq", "fsdp"),
        P("fsdp", "seq"),
        P("fsdp", None),
        P("seq", "fsdp"),
    )
    return jax.shard_map(
        on_device,
        mesh=mesh,
        in_specs=placed,
        out_specs=(
            P("seq", "fsdp"),
            P("seq", "fsdp"),
            P(None, "seq", "fsdp"),
            P("fsdp", "seq"),
            P("fsdp", None),
        ),
        check_vma=False,
    )
```

profile of v0, /device:TPU:16, one launch (start us, length us, event | category | flops | bytes accessed | tf_op | source)
XLA Modules:
  0.0 766.9 jit_solution(3096591360201777987)
XLA Ops:
  7.2 0.0 all-gather.7.cloned.1.call-start
  7.2 0.7 all-gather.7.cloned.1.call-update
  7.9 0.0 all-gather.5.cloned.1.call-start
  7.9 0.7 all-gather.5.cloned.1.call-update
  8.6 0.0 all-gather.11.cloned.1.call-start
  8.7 0.7 all-gather.11.cloned.1.call-update
  9.4 0.0 all-gather.9.cloned.1.call-start
  9.4 0.5 all-gather.9.cloned.1.call-update
  10.0 0.0 copy-start.3
  10.0 0.0 all-reduce.2.cloned.1.call-start
  10.0 38.7 %all-gather.7.cloned.1.call-done = bf16[128,4096]{1,0:T(8,128)(2,1)} async-done(((bf16[128,256]{1,0:T(8,128)(2,1)}), bf16[128,4096]{1,0:T(8,128)(2,1)}) %all-gather.7.cloned.1.call-update) | async-done | bytes 1048592 | tf_op jit(solution)/shard_map/all_gather | solution.py:58
  48.7 93.1 %all-gather.5.cloned.1.call-done = bf16[3,4096,256]{2,1,0:T(8,128)(2,1)} async-done(((bf16[3,256,256]{2,1,0:T(8,128)(2,1)}), bf16[3,4096,256]{2,1,0:T(8,128)(2,1)}) %all-gather.5.cloned.1.call-update) | async-done | bytes 6291472 | tf_op jit(solution)/shard_map/all_gather | solution.py:60
  141.8 4.1 fusion.2
  145.9 38.9 %all-gather.11.cloned.1.call-done = bf16[128,4096]{1,0:T(8,128)(2,1)} async-done(((bf16[128,256]{1,0:T(8,128)(2,1)}), bf16[128,4096]{1,0:T(8,128)(2,1)}) %all-gather.11.cloned.1.call-update) | async-done | bytes 1048592 | tf_op jit(solution)/shard_map/all_gather | solution.py:75
  184.8 64.7 %all-gather.9.cloned.1.call-done = bf16[256,4096]{1,0:T(8,128)(2,1)} async-done(((bf16[256,256]{1,0:T(8,128)(2,1)}), bf16[256,4096]{1,0:T(8,128)(2,1)}) %all-gather.9.cloned.1.call-update) | async-done | bytes 2097168 | tf_op jit(solution)/shard_map/all_gather | solution.py:59
  249.5 2.8 fusion.15
  252.3 3.5 collective-permute-start.1
  255.8 0.1 copy.13
  255.9 3.4 collective-permute-done.1
  259.4 1.4 fusion.5
  260.8 3.8 collective-permute-start
  264.7 0.2 rev.7
  264.9 0.1 copy.11
  265.0 5.0 collective-permute-done
  270.0 1.4 fusion.9
  271.5 1.9 fusion.7
  273.4 0.7 rev.8
  274.0 0.0 all-reduce.2.cloned.1.call-update
  274.1 0.0 reduce-scatter.11.cloned.1.call-start
  274.1 2.0 convolution_convert_fusion.1
  276.2 0.0 reduce-scatter.11.cloned.1.call-update
  276.2 0.0 reduce-scatter.9.cloned.1.call-start
  276.3 4.4 fusion
  280.7 0.0 reduce-scatter.9.cloned.1.call-update
  280.8 0.0 reduce-scatter.7.cloned.1.call-start
  280.8 6.0 fusion.1
  286.8 0.0 reduce-scatter.7.cloned.1.call-update
  286.9 0.0 reduce-scatter.5.cloned.1.call-start
  286.9 1.5 convolution_convert_fusion.2
  288.4 0.0 reduce-scatter.5.cloned.1.call-update
  288.4 137.5 %all-reduce.2.cloned.1.call-done = bf16[256,128]{0,1:T(8,128)(2,1)} async-done(((bf16[256,128]{0,1:T(8,128)(2,1)}), bf16[256,128]{0,1:T(8,128)(2,1)}) %all-reduce.2.cloned.1.call-update) | async-done | bytes 65552 | tf_op jit(solution)/shard_map/psum | solution.py:85
  425.9 1.6 copy.20
  427.5 87.5 %reduce-scatter.11.cloned.1.call-done = bf16[256,256]{1,0:T(8,128)(2,1)} async-done(((bf16[256,4096]{1,0:T(8,128)(2,1)}), bf16[256,256]{1,0:T(8,128)(2,1)}) %reduce-scatter.11.cloned.1.call-update) | async-done | bytes 131088 | tf_op jit(solution)/shard_map/reduce_scatter | solution.py:107
  515.1 1.6 convert_element_type.84
  516.7 110.3 %reduce-scatter.9.cloned.1.call-done = bf16[3,256,256]{1,2,0:T(8,128)(2,1)} async-done(((bf16[3,4096,256]{1,2,0:T(8,128)(2,1)}), bf16[3,256,256]{1,2,0:T(8,128)(2,1)}) %reduce-scatter.9.cloned.1.call-update) | async-done | bytes 393232 | tf_op jit(solution)/shard_map/reduce_scatter | solution.py:104
  627.0 2.0 copy.19
  629.0 65.3 %reduce-scatter.7.cloned.1.call-done = bf16[128,256]{1,0:T(8,128)(2,1)} async-done(((bf16[128,4096]{1,0:T(8,128)(2,1)}), bf16[128,256]{1,0:T(8,128)(2,1)}) %reduce-scatter.7.cloned.1.call-update) | async-done | bytes 65552 | tf_op jit(solution)/shard_map/reduce_scatter | solution.py:94
  694.3 66.1 %reduce-scatter.5.cloned.1.call-done = bf16[128,256]{1,0:T(8,128)(2,1)} async-done(((bf16[128,4096]{1,0:T(8,128)(2,1)}), bf16[128,256]{1,0:T(8,128)(2,1)}) %reduce-scatter.5.cloned.1.call-update) | async-done | bytes 65552 | tf_op jit(solution)/shard_map/reduce_scatter | solution.py:72
  (13 shorter events, 0.1 us)
Async XLA Ops:
  7.2 41.6 %all-gather.7.cloned.1.call-start = ((), (), s32[]{:S(2)}) async-start(), calls=%async_computation.5 | async-start | bytes 1114112 | tf_op jit(solution)/shard_map/all_gather | solution.py:58
  7.9 133.9 %all-gather.5.cloned.1.call-start = ((), (), s32[]{:S(2)}) async-start(), calls=%async_computation.4 | async-start | bytes 6684672 | tf_op jit(solution)/shard_map/all_gather | solution.py:60
  8.6 176.2 %all-gather.11.cloned.1.call-start = ((), (), s32[]{:S(2)}) async-start(), calls=%async_computation.8 | async-start | bytes 1114112 | tf_op jit(solution)/shard_map/all_gather | solution.py:75
  9.4 240.1 %all-gather.9.cloned.1.call-start = ((), (), s32[]{:S(2)}) async-start(), calls=%async_computation.6 | async-start | bytes 2228224 | tf_op jit(solution)/shard_map/all_gather | solution.py:59
  10.0 245.8 %copy-start.3 = (f32[256,128]{1,0:T(8,128)S(1)}, f32[256,128]{1,0:T(8,128)}, u32[]{:S(2)}) copy-start(f32[256,128]{1,0:T(8,128)} %param.8) | copy-start | bytes 393220
  10.0 416.0 %all-reduce.2.cloned.1.call-start = ((), (), s32[]{:S(2)}) async-start(), calls=%async_computation.12 | async-start | bytes 131072 | tf_op jit(solution)/shard_map/psum | solution.py:85
  252.3 7.1 collective-permute-start.1
  260.8 9.2 %collective-permute-start = (bf16[127,256]{1,0:T(8,128)(2,1)S(1)}, bf16[127,256]{1,0:T(8,128)(2,1)S(1)}, u32[]{:S(2)}, u32[]{:S(2)}) collective-permute-start(bf16[127,256]{1,0:T(8,128)(2,1)S(1)} %slice_bitcast_fusion), channel_id=1, source_target_pairs={{0,16},{16,32},{32,48},{48,64},{64,80},{80,96},{96,112},{112,128},... | collective-permute-start | bytes 195080 | tf_op jit(solution)/shard_map/ppermute | solution.py:12
  271.4 2.7 copy-start.2
  273.3 2.9 copy-start.1
  274.1 241.0 %reduce-scatter.11.cloned.1.call-start = ((), (), s32[]{:S(2)}) async-start(), calls=%async_computation.11 | async-start | bytes 2228224 | tf_op jit(solution)/shard_map/reduce_scatter | solution.py:107
  276.2 350.8 %reduce-scatter.9.cloned.1.call-start = ((), (), s32[]{:S(2)}) async-start(), calls=%async_computation.10 | async-start | bytes 6684672 | tf_op jit(solution)/shard_map/reduce_scatter | solution.py:104
  280.7 6.2 copy-start
  280.8 413.5 %reduce-scatter.7.cloned.1.call-start = ((), (), s32[]{:S(2)}) async-start(), calls=%async_computation.9 | async-start | bytes 1114112 | tf_op jit(solution)/shard_map/reduce_scatter | solution.py:94
  286.9 473.5 %reduce-scatter.5.cloned.1.call-start = ((), (), s32[]{:S(2)}) async-start(), calls=%async_computation.7 | async-start | bytes 1114112 | tf_op jit(solution)/shard_map/reduce_scatter | solution.py:72
Sparse Core Ops, SparseCore 0:
  9.7 38.9 all-gather.6
  51.2 90.5 all-gather.4
  143.6 41.1 all-gather.10
  187.1 62.4 all-gather.8
  274.2 151.6 all-reduce.1
  429.3 85.6 reduce-scatter.10
  518.8 108.1 reduce-scatter.8
  630.0 64.1 reduce-scatter.6
  697.4 62.9 reduce-scatter.4
where the time goes:
time: 767 us
  waiting for transfers between devices  713 us (93%)
  matrix products  25.5 us (3%)
  between operations  14 us (2%)
  starting transfers between devices  7.7 us (1%)
    psum x1, waiting for transfers between devices, on_device(): lax.psum(filter_grad(extended, grad_filtered.astype(jnp.float32)).astype(...  138 us
    reduce_scatter x1, waiting for transfers between devices, on_device(): lax.psum_scatter(weight_in_part.astype(jnp.bfloat16), 'seq', scatter_dime...  110 us
    all_gather x1, waiting for transfers between devices, on_device(): in_full = lax.all_gather(in_weight, 'seq', axis=1, tiled=True)  93.1 us
    reduce_scatter x1, waiting for transfers between devices, on_device(): lax.psum_scatter(weight_out_part.astype(jnp.bfloat16), 'seq', scatter_dim...  87.5 us
    reduce_scatter x1, waiting for transfers between devices, on_device(): lax.psum_scatter(partial_value.astype(jnp.bfloat16), 'fsdp', scatter_dime...  66.1 us
    reduce_scatter x1, waiting for transfers between devices, on_device(): lax.psum_scatter(grad_partial.astype(jnp.bfloat16), 'fsdp', scatter_dimen...  65.3 us
    all_gather x1, waiting for transfers between devices, on_device(): out_full = lax.all_gather(out_weight, 'seq', axis=1, tiled=True)  64.7 us
    all_gather x1, waiting for transfers between devices, on_device(): grad_full = lax.all_gather(cotangent, 'fsdp', axis=1, tiled=True)  38.9 us
  transfers between devices with their start and end apart: 11, of which 11 were waited for; matrix products, arithmetic and copies ran while one was open for 3% of the time, Pallas kernels for 0%

commit v1 on v0

--- a/solution.py
+++ b/solution.py
@@ -4,6 +4,11 @@
 from jax.sharding import PartitionSpec as P
 
 highest = lax.Precision.HIGHEST
+
+
+def enter_object_by_axis(obj, axis_tag):
+    arr_now = lax.all_to_all(jnp.stack(lax.axis_size(axis_tag) * [obj], axis=0), axis_tag, 0, 0)
+    return jnp.concatenate(arr_now, axis=1)
 
 
 def from_behind(value, axis, by):
@@ -56,7 +61,7 @@
 def on_device(tokens, in_weight, out_weight, filters, cotangent):
     margin = filters.shape[1] - 1
     gathered = lax.all_gather(tokens, "fsdp", axis=1, tiled=True)
-    out_full = lax.all_gather(out_weight, "seq", axis=1, tiled=True)
+    out_full = enter_object_by_axis(out_weight, "seq")
     in_full = lax.all_gather(in_weight, "seq", axis=1, tiled=True)
     projected = jnp.einsum("td,idc->itc", gathered, in_full, preferred_element_type=jnp.float32)
     projected = projected.astype(jnp.bfloat16)

time: 767 us -> 722 us (0.941)
  waiting for transfers between devices: 713 us -> 646 us
  starting transfers between devices: 7.7 us -> 22.7 us
    all_gather x1 -> x0, waiting for transfers between devices: 64.7 us -> none  [on_device(): out_full = lax.all_gather(out_weight, 'seq', axis=1, tiled=True)]
    all_to_all x0 -> x1, starting transfers between devices: none -> 11.4 us  [enter_object_by_axis(): lax.all_to_all(jnp.stack(lax.axis_size(axis_tag) * [obj], axis=0), axis_t...]
  transfers between devices with their start and end apart: 11 -> 11, of which waited for: 11 -> 10; matrix products, arithmetic and copies ran while one was open for 3% -> 4% of each run, Pallas kernels for 0% -> 0%
where the time goes in v1:
time: 722 us
  waiting for transfers between devices  646 us (89%)
  matrix products  27.5 us (4%)
  starting transfers between devices  22.7 us (3%)
  between operations  14.3 us (2%)
  local copies, waits for them, and re-layouts  8 us (1%)
    psum x1, waiting for transfers between devices, on_device(): lax.psum(filter_grad(extended, grad_filtered.astype(jnp.float32)).astype(...  135 us
    reduce_scatter x1, waiting for transfers between devices, on_device(): lax.psum_scatter(weight_in_part.astype(jnp.bfloat16), 'seq', scatter_dime...  110 us
    all_gather x1, waiting for transfers between devices, on_device(): in_full = lax.all_gather(in_weight, 'seq', axis=1, tiled=True)  96.3 us
    reduce_scatter x1, waiting for transfers between devices, on_device(): lax.psum_scatter(weight_out_part.astype(jnp.bfloat16), 'seq', scatter_dim...  87.7 us
    reduce_scatter x1, waiting for transfers between devices, on_device(): lax.psum_scatter(grad_partial.astype(jnp.bfloat16), 'fsdp', scatter_dimen...  65.9 us
    reduce_scatter x1, waiting for transfers between devices, on_device(): lax.psum_scatter(partial_value.astype(jnp.bfloat16), 'fsdp', scatter_dime...  65.1 us
    all_gather x1, waiting for transfers between devices, on_device(): grad_full = lax.all_gather(cotangent, 'fsdp', axis=1, tiled=True)  38.9 us
    all_gather x1, waiting for transfers between devices, on_device(): gathered = lax.all_gather(tokens, 'fsdp', axis=1, tiled=True)  37.4 us
  transfers between devices with their start and end apart: 11, of which 10 were waited for; matrix products, arithmetic and copies ran while one was open for 4% of the time, Pallas kernels for 0%

profile of v1, /device:TPU:16, one launch (start us, length us, event | category | flops | bytes accessed | tf_op | source)
XLA Modules:
  0.0 721.6 jit_solution(14588080221168039738)
XLA Ops:
  7.2 0.0 all-gather.6.cloned.1.call-start
  7.2 0.7 all-gather.6.cloned.1.call-update
  7.9 0.0 all-gather.4.cloned.1.call-start
  7.9 0.7 all-gather.4.cloned.1.call-update
  8.6 1.0 copy.25
  9.7 1.6 stack.8
  11.2 11.4 %all-to-all-start = ((bf16[16,256,256]{1,2,0:T(8,128)(2,1)}), bf16[16,256,256]{1,2,0:T(8,128)(2,1)S(1)}, u32[]{:S(2)}, u32[]{:S(2)}) async-start(bf16[16,256,256]{1,2,0:T(8,128)(2,1)} %stack.8), calls=%async_computation | async-start | bytes 4194304 | tf_op jit(solution)/shard_map/all_to_all | solution.py:10
  22.7 0.0 all-gather.8.cloned.1.call-start
  22.7 0.7 all-gather.8.cloned.1.call-update
  23.4 0.0 all-reduce.2.cloned.1.call-start
  23.4 37.4 %all-gather.6.cloned.1.call-done = bf16[128,4096]{1,0:T(8,128)(2,1)} async-done(((bf16[128,256]{1,0:T(8,128)(2,1)}), bf16[128,4096]{1,0:T(8,128)(2,1)}) %all-gather.6.cloned.1.call-update) | async-done | bytes 1048592 | tf_op jit(solution)/shard_map/all_gather | solution.py:63
  60.9 96.3 %all-gather.4.cloned.1.call-done = bf16[3,4096,256]{2,1,0:T(8,128)(2,1)} async-done(((bf16[3,256,256]{2,1,0:T(8,128)(2,1)}), bf16[3,4096,256]{2,1,0:T(8,128)(2,1)}) %all-gather.4.cloned.1.call-update) | async-done | bytes 6291472 | tf_op jit(solution)/shard_map/all_gather | solution.py:65
  157.1 4.1 fusion.2
  161.3 38.9 %all-gather.8.cloned.1.call-done = bf16[128,4096]{1,0:T(8,128)(2,1)} async-done(((bf16[128,256]{1,0:T(8,128)(2,1)}), bf16[128,4096]{1,0:T(8,128)(2,1)}) %all-gather.8.cloned.1.call-update) | async-done | bytes 1048592 | tf_op jit(solution)/shard_map/all_gather | solution.py:80
  200.1 2.3 fusion.13
  202.5 5.7 collective-permute-start.1
  208.2 0.1 copy.27
  208.4 3.0 collective-permute-done.1
  211.4 1.4 fusion.5
  212.8 0.7 fusion.18
  213.5 5.2 collective-permute-start
  218.7 0.2 rev.7
  218.9 0.1 copy.23
  219.0 4.1 collective-permute-done
  223.1 1.4 fusion.9
  224.5 1.9 fusion.7
  226.4 0.7 rev.8
  227.1 0.0 all-reduce.2.cloned.1.call-update
  227.2 0.0 reduce-scatter.11.cloned.1.call-start
  227.2 3.4 convolution_convert_fusion.1
  230.6 0.0 reduce-scatter.11.cloned.1.call-update
  230.6 0.0 reduce-scatter.9.cloned.1.call-start
  230.7 0.9 fusion.21
  231.6 0.6 copy-done.2
  232.2 5.3 fusion
  237.5 0.0 reduce-scatter.9.cloned.1.call-update
  237.5 0.0 reduce-scatter.5.cloned.1.call-start
  237.6 1.8 convolution_convert_fusion.2
  239.4 0.0 reduce-scatter.7.cloned.1.call-start
  239.5 5.9 fusion.1
  245.4 135.0 %all-reduce.2.cloned.1.call-done = bf16[256,128]{0,1:T(8,128)(2,1)} async-done(((bf16[256,128]{0,1:T(8,128)(2,1)}), bf16[256,128]{0,1:T(8,128)(2,1)}) %all-reduce.2.cloned.1.call-update) | async-done | bytes 65552 | tf_op jit(solution)/shard_map/psum | solution.py:90
  380.4 1.6 copy.34
  382.0 87.7 %reduce-scatter.11.cloned.1.call-done = bf16[256,256]{1,0:T(8,128)(2,1)} async-done(((bf16[256,4096]{1,0:T(8,128)(2,1)}), bf16[256,256]{1,0:T(8,128)(2,1)}) %reduce-scatter.11.cloned.1.call-update) | async-done | bytes 131088 | tf_op jit(solution)/shard_map/reduce_scatter | solution.py:112
  469.7 1.6 convert_element_type.95
  471.3 110.4 %reduce-scatter.9.cloned.1.call-done = bf16[3,256,256]{1,2,0:T(8,128)(2,1)} async-done(((bf16[3,4096,256]{1,2,0:T(8,128)(2,1)}), bf16[3,256,256]{1,2,0:T(8,128)(2,1)}) %reduce-scatter.9.cloned.1.call-update) | async-done | bytes 393232 | tf_op jit(solution)/shard_map/reduce_scatter | solution.py:109
  581.7 2.0 copy.33
  583.8 65.1 %reduce-scatter.5.cloned.1.call-done = bf16[128,256]{1,0:T(8,128)(2,1)} async-done(((bf16[128,4096]{1,0:T(8,128)(2,1)}), bf16[128,256]{1,0:T(8,128)(2,1)}) %reduce-scatter.5.cloned.1.call-update) | async-done | bytes 65552 | tf_op jit(solution)/shard_map/reduce_scatter | solution.py:77
  648.9 65.9 %reduce-scatter.7.cloned.1.call-done = bf16[128,256]{1,0:T(8,128)(2,1)} async-done(((bf16[128,4096]{1,0:T(8,128)(2,1)}), bf16[128,256]{1,0:T(8,128)(2,1)}) %reduce-scatter.7.cloned.1.call-update) | async-done | bytes 65552 | tf_op jit(solution)/shard_map/reduce_scatter | solution.py:99
  (16 shorter events, 0.1 us)
Async XLA Ops:
  7.2 53.7 %all-gather.6.cloned.1.call-start = ((), (), s32[]{:S(2)}) async-start(), calls=%async_computation.6 | async-start | bytes 1114112 | tf_op jit(solution)/shard_map/all_gather | solution.py:63
  7.9 149.2 %all-gather.4.cloned.1.call-start = ((), (), s32[]{:S(2)}) async-start(), calls=%async_computation.5 | async-start | bytes 6684672 | tf_op jit(solution)/shard_map/all_gather | solution.py:65
  11.2 188.9 %all-to-all-start = ((bf16[16,256,256]{1,2,0:T(8,128)(2,1)}), bf16[16,256,256]{1,2,0:T(8,128)(2,1)S(1)}, u32[]{:S(2)}, u32[]{:S(2)}) async-start(bf16[16,256,256]{1,2,0:T(8,128)(2,1)} %stack.8), calls=%async_computation | async-start | bytes 4194304 | tf_op jit(solution)/shard_map/all_to_all | solution.py:10
  22.7 177.5 %all-gather.8.cloned.1.call-start = ((), (), s32[]{:S(2)}) async-start(), calls=%async_computation.8 | async-start | bytes 1114112 | tf_op jit(solution)/shard_map/all_gather | solution.py:80
  23.4 357.0 %all-reduce.2.cloned.1.call-start = ((), (), s32[]{:S(2)}) async-start(), calls=%async_computation.12 | async-start | bytes 131072 | tf_op jit(solution)/shard_map/psum | solution.py:90
  161.2 47.0 %copy-start.4 = (f32[256,128]{1,0:T(8,128)S(1)}, f32[256,128]{1,0:T(8,128)}, u32[]{:S(2)}) copy-start(f32[256,128]{1,0:T(8,128)} %param.8) | copy-start | bytes 393220
  202.5 8.9 %collective-permute-start.1 = (bf16[127,256]{1,0:T(8,128)(2,1)S(1)}, bf16[127,256]{1,0:T(8,128)(2,1)S(1)}, u32[]{:S(2)}, u32[]{:S(2)}) collective-permute-start(bf16[127,256]{1,0:T(8,128)(2,1)S(1)} %bitcast.75), channel_id=1, source_target_pairs={{16,0},{32,16},{48,32},{64,48},{80,64},{96,80},{112,96},{128,112},... | collective-permute-start | bytes 195080 | tf_op jit(solution)/shard_map/ppermute | solution.py:17
  213.5 9.6 %collective-permute-start = (bf16[127,256]{1,0:T(8,128)(2,1)S(1)}, bf16[127,256]{1,0:T(8,128)(2,1)S(1)}, u32[]{:S(2)}, u32[]{:S(2)}) collective-permute-start(bf16[127,256]{1,0:T(8,128)(2,1)S(1)} %slice_bitcast_fusion), channel_id=1, source_target_pairs={{0,16},{16,32},{32,48},{48,64},{64,80},{80,96},{96,112},{112,128},... | collective-permute-start | bytes 195080 | tf_op jit(solution)/shard_map/ppermute | solution.py:17
  227.1 5.1 copy-start
  227.2 242.5 %reduce-scatter.11.cloned.1.call-start = ((), (), s32[]{:S(2)}) async-start(), calls=%async_computation.11 | async-start | bytes 2228224 | tf_op jit(solution)/shard_map/reduce_scatter | solution.py:112
  230.6 351.1 %reduce-scatter.9.cloned.1.call-start = ((), (), s32[]{:S(2)}) async-start(), calls=%async_computation.10 | async-start | bytes 6684672 | tf_op jit(solution)/shard_map/reduce_scatter | solution.py:109
  231.6 0.6 copy-start.2
  237.5 2.0 copy-start.1
  237.5 2.0 copy-start.3
  237.5 411.3 %reduce-scatter.5.cloned.1.call-start = ((), (), s32[]{:S(2)}) async-start(), calls=%async_computation.7 | async-start | bytes 1114112 | tf_op jit(solution)/shard_map/reduce_scatter | solution.py:77
  239.4 475.3 %reduce-scatter.7.cloned.1.call-start = ((), (), s32[]{:S(2)}) async-start(), calls=%async_computation.9 | async-start | bytes 1114112 | tf_op jit(solution)/shard_map/reduce_scatter | solution.py:99
Sparse Core Ops, SparseCore 0:
  9.7 51.0 all-gather.5
  63.4 93.7 all-gather.3
  158.9 41.1 all-gather.7
  227.3 153.0 all-reduce.1
  383.8 85.8 reduce-scatter.10
  473.3 108.4 reduce-scatter.8
  584.8 64.0 reduce-scatter.4
  652.0 62.7 reduce-scatter.6
